TPU v7x, 32 devices: a whole 2x2x4 slice. The times are simulated.
32 devices in a mesh: group: 2 (over x), row: 8 (over z, y), tp: 2 (over core).
Axes of the slice: x: 2, y: 2, z: 4, core: 2. Of those that a mesh axis runs over, the one named last changes fastest.
Arguments:
- prompt_latent: bfloat16 [16, 16, 128, 576], P(('group', 'row'), None, 'tp'), parts along dimension 0, may hold values from -6 to 6
- row_cache: bfloat16 [32, 256, 576], P(('group', 'row')), parts along dimension 0, may hold values from -24 to 24
- queries: bfloat16 [4, 32, 128, 576], P(None, ('group', 'row'), 'tp'), parts along dimension 1, may hold values from -80 to 80
- new_latent: bfloat16 [4, 32, 576], P(None, ('group', 'row')), parts along dimension 1, may hold values from -12 to 12
- prompt_len: int32 [32], P('group'), parts along dimension 0, may hold values from 1 to 1024, 12288 in all
- assign: int32 [32], P('group'), parts along dimension 0, may hold values from 0 to 15, as said below
- row_ctx: int32 [32], P(('group', 'row')), parts along dimension 0, may hold values from 2 to 256
Outputs:
- attended: bfloat16 [4, 32, 128, 512], P(None, ('group', 'row'), 'tp'), parts along dimension 1
There are 2 independent parts, one for each index of `group`. A program takes and returns all parts, laid end to end along the dimension named above; each array names one. Nothing has to cross between parts.
Inputs may be any that keep to these rules, and one draw needn't show every extreme that they name: `prompt_len`: latents at positions from a prompt's length on are not part of that prompt. Decode row r continues prompt assign[r]; every prompt goes to exactly one row. Prompt p belongs to prompt group p // 16; the rows of one index of row take at most 2 prompts of any one prompt group. Row r's cached latents are its first row_ctx[r] positions.
All inputs are finite; a program needn't handle non-finite values.
Results may differ from a plain program's by a relative error of at most 0.0044.
Values may be sent and summed in bfloat16 or wider, within the bound.
No kernel may reach another device: no remote copies, remote signals or barrier semaphores. Data moves between devices by JAX's collectives and lax.ppermute only.
A program may use at most 128 MiB of HBM per device.

v0:
```python
import functools

import jax
import jax.numpy as jnp
from jax import lax
from jax.experimental import pallas as pl
from jax.experimental.pallas import tpu as pltpu
from jax.sharding import PartitionSpec as P


KV_RANK = 512
ROPE_DIM = 64
NOPE_DIM = 128
SPR = 8
LANES = 128

PACK_VMEM = 4 << 20
ATTEND_VMEM = 16 << 20

SEND_ORDER = (4, 5, 2, 3, 11, 10, 6)
STAGES = ((0,), (4, 5), (2, 3, 11), (10, 6))
ROUNDS = sum(STAGES, ())
MIXED = {10: (7, 1), 11: (1, 7)}


def partner(number, place):
    if number not in MIXED:
        return place ^ number
    inner, outer = MIXED[number]
    middle = ((place >> 1) ^ (place >> 2)) & 1
    return place ^ (middle * inner + (1 - middle) * outer)


def write_bias(bias_ref, lives, caches, place, side, piece):
    block = 2 * piece
    rows, keys, lanes = bias_ref.shape
    slot = lax.broadcasted_iota(jnp.int32, (block, lanes), 0)
    spot = jnp.where(slot < piece, side * piece + slot, (1 - side) * piece + slot - piece)
    kept = lax.broadcasted_iota(jnp.int32, (keys - SPR * block, lanes), 0)
    for r in range(rows):
        for i, number in enumerate(ROUNDS):
            live = spot + partner(number, place) * block < lives[r]
            bias_ref[r, i * block : (i + 1) * block] = jnp.where(live, 0.0, -jnp.inf)
        bias_ref[r, SPR * block :] = jnp.where(kept < caches[r], 0.0, -jnp.inf)


def join_rows(rows):
    return jnp.concatenate(
        [row[:, :KV_RANK] for row in rows] + [row[:, KV_RANK:] for row in rows], axis=1
    )


def pack_kernel(order, rows_here, assign_hbm, latent_hbm, *refs):
    outs, (assign_ref, latent_ref, sems) = refs[: len(order)], refs[len(order) :]
    copies = [
        pltpu.make_async_copy(assign_hbm, assign_ref, sems.at[0]),
        pltpu.make_async_copy(latent_hbm, latent_ref, sems.at[1]),
    ]
    for copy in copies:
        copy.start()
    for copy in copies:
        copy.wait()
    place = lax.axis_index("row")
    for out, offset in zip(outs, order):
        first = partner(offset, place) * rows_here
        out[...] = join_rows([latent_ref[assign_ref[first + r]] for r in range(rows_here)])


def in_hbm(*arrays):
    return [pltpu.with_memory_space_constraint(x, pltpu.HBM) for x in arrays]


def pack(order, assign, local, rows_here):
    _, piece, width = local.shape
    vmem = pl.BlockSpec(memory_space=pltpu.VMEM)
    out = pl.pallas_call(
        functools.partial(pack_kernel, order, rows_here),
        out_shape=[jax.ShapeDtypeStruct((piece, rows_here * width), local.dtype) for _ in order],
        in_specs=[pl.BlockSpec(memory_space=pltpu.HBM)] * 2,
        out_specs=[vmem] * len(order),
        scratch_shapes=[
            pltpu.SMEM(assign.shape, jnp.int32),
            pltpu.VMEM(local.shape, local.dtype),
            pltpu.SemaphoreType.DMA((2,)),
        ],
        compiler_params=pltpu.CompilerParams(vmem_limit_bytes=PACK_VMEM),
        name="pack",
    )(*in_hbm(assign, local))
    return dict(zip(order, out))


def bias_kernel(piece, assign_hbm, length_hbm, ctx_hbm, bias_ref, assign_ref, length_ref, ctx_ref, sems):
    copies = [
        pltpu.make_async_copy(src, dst, sems.at[i])
        for i, (src, dst) in enumerate(
            ((assign_hbm, assign_ref), (length_hbm, length_ref), (ctx_hbm, ctx_ref))
        )
    ]
    for copy in copies:
        copy.start()
    for copy in copies:
        copy.wait()
    rows_here = ctx_hbm.shape[0]
    place, side = lax.axis_index("row"), lax.axis_index("tp")
    lives = [length_ref[assign_ref[place * rows_here + r]] for r in range(rows_here)]
    caches = [ctx_ref[r] for r in range(rows_here)]
    write_bias(bias_ref, lives, caches, place, side, piece)


def make_bias(assign, prompt_len, row_ctx, piece, cached):
    shape = (row_ctx.shape[0], SPR * 2 * piece + cached, LANES)
    return pl.pallas_call(
        functools.partial(bias_kernel, piece),
        out_shape=jax.ShapeDtypeStruct(shape, jnp.float32),
        in_specs=[pl.BlockSpec(memory_space=pltpu.HBM)] * 3,
        out_specs=pl.BlockSpec(memory_space=pltpu.VMEM),
        scratch_shapes=[
            pltpu.SMEM(assign.shape, jnp.int32),
            pltpu.SMEM(prompt_len.shape, jnp.int32),
            pltpu.SMEM(row_ctx.shape, jnp.int32),
            pltpu.SemaphoreType.DMA((3,)),
        ],
        compiler_params=pltpu.CompilerParams(vmem_limit_bytes=PACK_VMEM),
        name="bias",
    )(*in_hbm(assign, prompt_len, row_ctx))


def spread_kernel(q_hbm, cache_hbm, out_ref, cache_ref, q_ref, sems):
    copies = [
        pltpu.make_async_copy(q_hbm, q_ref, sems.at[0]),
        pltpu.make_async_copy(cache_hbm, cache_ref, sems.at[1]),
    ]
    for copy in copies:
        copy.start()
    copies[0].wait()
    steps, rows, heads, width = q_ref.shape
    rope = width - KV_RANK
    for r in range(rows):
        query = q_ref[:, r].reshape(steps * heads, width)
        out_ref[r, :, :KV_RANK] = query[:, :KV_RANK]
        blank = jnp.zeros((steps * heads, rope), query.dtype)
        tail = [query[:, KV_RANK:] if other == r else blank for other in range(rows)]
        out_ref[r, :, KV_RANK:] = jnp.concatenate(tail, axis=1)
    copies[1].wait()


def spread_queries(queries, turned):
    steps, rows, heads, width = queries.shape
    wide = KV_RANK + rows * (width - KV_RANK)
    hbm, vmem = pl.BlockSpec(memory_space=pltpu.HBM), pl.BlockSpec(memory_space=pltpu.VMEM)
    return pl.pallas_call(
        spread_kernel,
        out_shape=[
            jax.ShapeDtypeStruct((rows, steps * heads, wide), queries.dtype),
            jax.ShapeDtypeStruct(turned.shape, turned.dtype),
        ],
        in_specs=[hbm] * 2,
        out_specs=[vmem] * 2,
        scratch_shapes=[
            pltpu.VMEM(queries.shape, queries.dtype),
            pltpu.SemaphoreType.DMA((2,)),
        ],
        compiler_params=pltpu.CompilerParams(vmem_limit_bytes=PACK_VMEM),
        name="spread",
    )(*in_hbm(queries, turned))


def attend_kernel(offsets, heads, first, last, bias_ref, q_ref, *refs):
    refs = list(refs)
    own = [refs.pop(0) for _ in offsets]
    other = [refs.pop(0) for _ in offsets]
    if first:
        cache_ref, new_ref = refs.pop(0), refs.pop(0)
    else:
        top_in, sum_in, acc_in = refs.pop(0), refs.pop(0), refs.pop(0)
    if last:
        out_ref, stage_ref, sems = refs
    else:
        top_out, sum_out, acc_out = refs
    rows, tall, _ = q_ref.shape
    piece = own[0].shape[0]
    block = 2 * piece
    scale = (NOPE_DIM + ROPE_DIM) ** -0.5
    by_width = (((1,), (1,)), ((), ()))
    by_key = (((0,), (0,)), ((), ()))
    dot = functools.partial(lax.dot_general, preferred_element_type=jnp.float32)

    def mask(r, start, count):
        return jnp.concatenate([bias_ref[r, start : start + count]] * (tall // LANES), axis=1)

    def column(line):
        turned = jnp.broadcast_to(line, (LANES, tall)).T
        return jnp.concatenate([turned] * (KV_RANK // LANES), axis=1)

    every = range(rows)
    halves = [half for pair in zip(own, other) for half in pair]
    value = [
        jnp.concatenate([h[:, r * KV_RANK : (r + 1) * KV_RANK] for h in halves], axis=0)
        for r in every
    ]
    rotary = jnp.concatenate([h[:, rows * KV_RANK :] for h in halves], axis=0)
    scores = []
    for r in every:
        found = dot(jnp.concatenate([value[r], rotary], axis=1), q_ref[r], by_width)
        biases = [mask(r, ROUNDS.index(number) * block, block) for number in offsets]
        scores.append([found * scale + jnp.concatenate(biases, axis=0)])
        if first:
            rope = new_ref.shape[2] - KV_RANK
            turn = q_ref[r, :, KV_RANK + r * rope : KV_RANK + (r + 1) * rope]
            narrow = jnp.concatenate([q_ref[r, :, :KV_RANK], turn], axis=1)
            cached = dot(cache_ref[r], narrow, (((0,), (1,)), ((), ())))
            scores[r].append(cached * scale + mask(r, SPR * block, cached.shape[0]))
            fresh = dot(new_ref[r], narrow, by_width)
            step = lax.broadcasted_iota(jnp.int32, fresh.shape, 1) // heads
            slot = lax.broadcasted_iota(jnp.int32, fresh.shape, 0)
            scores[r].append(jnp.where(slot <= step, fresh * scale, -jnp.inf))
    weights, shrinks = [], []
    for r in every:
        tops = [jnp.max(part, axis=0, keepdims=True) for part in scores[r]]
        if not first:
            tops.append(top_in[r])
        top = functools.reduce(jnp.maximum, tops)
        parts = [jnp.exp(part - top) for part in scores[r]]
        total = sum(jnp.sum(part, axis=0, keepdims=True) for part in parts)
        if not first:
            shrinks.append(jnp.exp(top_in[r] - top))
            total += shrinks[r] * sum_in[r]
        if last:
            share = 1.0 / total
            parts = [part * share for part in parts]
            shrinks[r] = shrinks[r] * share
        else:
            top_out[r] = top
            sum_out[r] = total
        weights.append([part.astype(q_ref.dtype) for part in parts])
    copies = []
    for r in every:
        acc = dot(weights[r][0], value[r], by_key)
        if first:
            acc += dot(weights[r][1].T, cache_ref[r, :KV_RANK], by_width)
            acc += dot(weights[r][2], new_ref[r, :, :KV_RANK], by_key)
        else:
            acc += column(shrinks[r]) * acc_in[r]
        if last:
            stage_ref[r] = acc.astype(out_ref.dtype).reshape(tall // heads, heads, KV_RANK)
            copies.append(
                pltpu.make_async_copy(stage_ref.at[r], out_ref.at[:, r], sems.at[r])
            )
            copies[r].start()
        else:
            acc_out[r] = acc
    for copy in copies:
        copy.wait()


def attend(offsets, bias, wide, own, other, shape, cache, fresh, carry, last):
    rows, tall, width = wide.shape
    steps, heads = shape[0], shape[2]
    first = carry is None
    keys = 2 * own[0].shape[0] * len(offsets)
    state = (
        jax.ShapeDtypeStruct((rows, 1, tall), jnp.float32),
        jax.ShapeDtypeStruct((rows, 1, tall), jnp.float32),
        jax.ShapeDtypeStruct((rows, tall, KV_RANK), jnp.float32),
    )
    final = (steps, rows, heads, KV_RANK)
    operands = (bias, wide, *own, *other, *((cache, fresh) if first else carry))
    vmem, hbm = pl.BlockSpec(memory_space=pltpu.VMEM), pl.BlockSpec(memory_space=pltpu.HBM)
    scratch = []
    if last:
        scratch = [
            pltpu.VMEM((rows, steps, heads, KV_RANK), wide.dtype),
            pltpu.SemaphoreType.DMA((rows,)),
        ]
    return pl.pallas_call(
        functools.partial(attend_kernel, offsets, heads, first, last),
        out_shape=jax.ShapeDtypeStruct(final, wide.dtype) if last else state,
        in_specs=[vmem] * len(operands),
        out_specs=hbm if last else (vmem,) * 3,
        scratch_shapes=scratch,
        cost_estimate=pl.CostEstimate(
            flops=2 * rows * tall * keys * (width + KV_RANK),
            bytes_accessed=2 * rows * (keys + tall) * width,
            transcendentals=rows * tall * keys,
        ),
        compiler_params=pltpu.CompilerParams(vmem_limit_bytes=ATTEND_VMEM),
        name="attend_last" if last else "attend",
    )(*operands)


def spread_exchange(local, assign, row_place, row_count, rows_here):
    group_rows = local.shape[0]
    most_slots = min(rows_here, max(2, 2 * rows_here * SPR // row_count))
    home_group = row_place // SPR
    dest_prompt = assign.reshape(row_count, rows_here)
    in_group = dest_prompt // group_rows == home_group
    rank = jnp.cumsum(in_group.astype(jnp.int32), axis=1) - 1
    slot_ids = jnp.arange(most_slots, dtype=jnp.int32)
    picked = in_group[:, :, None] & (rank[:, :, None] == slot_ids[None, None, :])
    local_id = dest_prompt - home_group * group_rows
    source_index = jnp.sum(jnp.where(picked, local_id[:, :, None], 0), axis=1)
    rows_taken = jnp.take(local, source_index.reshape(-1), axis=0)
    moved = lax.all_to_all(
        rows_taken.reshape((row_count, most_slots) + local.shape[1:]),
        "row",
        split_axis=0,
        concat_axis=0,
        tiled=True,
    )
    owned = lax.dynamic_slice_in_dim(assign, row_place * rows_here, rows_here)
    owned_group = owned // group_rows
    row_ids = jnp.arange(rows_here, dtype=jnp.int32)
    same_before = (owned_group[:, None] == owned_group[None, :]) & (
        row_ids[None, :] < row_ids[:, None]
    )
    own_rank = jnp.sum(same_before.astype(jnp.int32), axis=1)
    flat = moved.reshape((row_count * most_slots,) + local.shape[1:])
    place = row_place % SPR
    chunks = {}
    for offset in ROUNDS:
        index = (owned_group * SPR + partner(offset, place)) * most_slots + own_rank
        taken = jnp.take(flat, index, axis=0)
        chunks[offset] = join_rows([taken[r] for r in range(rows_here)])
    return chunks


def spread_bias(assign, prompt_len, row_ctx, row_place, side, piece, cached):
    rows_here = row_ctx.shape[0]
    owned = lax.dynamic_slice_in_dim(assign, row_place * rows_here, rows_here)
    lives = jnp.take(prompt_len, owned)
    lane = jnp.arange(2 * piece, dtype=jnp.int32)
    spot = jnp.where(lane < piece, side * piece + lane, (1 - side) * piece + lane - piece)
    block = jnp.stack([partner(number, row_place % SPR) for number in ROUNDS])
    spots = (spot[None, :] + block[:, None] * 2 * piece).reshape(1, -1)
    slots = jnp.arange(cached, dtype=jnp.int32)[None, :]
    live = jnp.concatenate([spots < lives[:, None], slots < row_ctx[:, None]], axis=1)
    bias = jnp.where(live, 0.0, -jnp.inf).astype(jnp.float32)
    return jnp.broadcast_to(bias[:, :, None], bias.shape + (LANES,))


def shards(prompt_latent, row_cache, queries, new_latent, prompt_len, assign, row_ctx):
    row_count = lax.axis_size("row")
    rows_here, cached = row_cache.shape[:2]
    local = prompt_latent[0]
    if row_count == SPR:
        packed = pack(SEND_ORDER + (0,), assign, local, rows_here)
        bias = make_bias(assign, prompt_len, row_ctx, local.shape[1], cached)
        mine = {0: packed[0]}
        for offset in SEND_ORDER:
            pairs = [(i, partner(offset, i)) for i in range(row_count)]
            mine[offset] = lax.ppermute(packed[offset], "row", pairs)
    else:
        row_place, side = lax.axis_index("row"), lax.axis_index("tp")
        mine = spread_exchange(local, assign, row_place, row_count, rows_here)
        bias = spread_bias(assign, prompt_len, row_ctx, row_place, side, local.shape[1], cached)
    theirs = {}
    for stage in STAGES:
        for offset in stage:
            theirs[offset] = lax.ppermute(mine[offset], "tp", [(0, 1), (1, 0)])
    fresh = jnp.swapaxes(new_latent, 0, 1)
    wide, turned = spread_queries(queries, jnp.swapaxes(row_cache, 1, 2))
    carry = None
    for number, stage in enumerate(STAGES):
        own, other = [mine[offset] for offset in stage], [theirs[offset] for offset in stage]
        last = number == len(STAGES) - 1
        carry = attend(
            stage, bias, wide, own, other, queries.shape, turned, fresh, carry, last
        )
    return carry


def solution(mesh):
    return jax.shard_map(
        shards,
        mesh=mesh,
        in_specs=(
            P(("group", "row"), None, "tp", None),
            P(("group", "row"), None, None),
            P(None, ("group", "row"), "tp", None),
            P(None, ("group", "row"), None),
            P("group"),
            P("group"),
            P(("group", "row")),
        ),
        out_specs=P(None, ("group", "row"), "tp", None),
        check_vma=False,
    )
```

profile of v0, /device:TPU:21, one launch (start us, length us, event | category | flops | bytes accessed | tf_op | source)
XLA Modules:
  0.0 39.0 jit_solution(1491376634638404361)
XLA Ops:
  0.0 1.5 %pack.1 = (bf16[64,1152]{1,0:T(8,128)(2,1)S(1)}, bf16[64,1152]{1,0:T(8,128)(2,1)S(1)}, bf16[64,1152]{1,0:T(8,128)(2,1)S(1)}, bf16[64,1152]{1,0:T(8,128)(2,1)S(1)...) custom-call(s32[16]{0:T(128)} %assign_hbm.3, ...), custom_call_target="tpu_custom_call" | custom-call | tf_op jit(solution)/shard_map/pack/pallas_call | solution.py:76
  1.5 0.7 %collective-permute-start.14 = (bf16[64,1152]{1,0:T(8,128)(2,1)S(1)}, bf16[64,1152]{1,0:T(8,128)(2,1)S(1)}, u32[]{:S(2)}, u32[]{:S(2)}) collective-permute-start(bf16[64,1152]{1,0:T(8,128)(2,1)S(1)} %get-tuple-element.32.refs_0_), channel_id=1, source_target_pairs={{0,1},{1,0},{2,3},{3,2},{4,5},{5,4},{6,7},{7,6},{8,9},{9,8},{10,11... | collective-permute-start | bytes 442376 | tf_op jit(solution)/shard_map/ppermute | solution.py:359
  2.3 2.3 %collective-permute-start.11 = (bf16[64,1152]{1,0:T(8,128)(2,1)S(1)}, bf16[64,1152]{1,0:T(8,128)(2,1)S(1)}, u32[]{:S(2)}, u32[]{:S(2)}) collective-permute-start(bf16[64,1152]{1,0:T(8,128)(2,1)S(1)} %get-tuple-element.31), channel_id=1, source_target_pairs={{0,10},{2,8},{4,14},{6,12},{8,2},{10,0},{12,6},{14,4},{1,11},{3,9}... | collective-permute-start | bytes 442376 | tf_op jit(solution)/shard_map/ppermute | solution.py:351
  4.5 1.3 %collective-permute-start.4 = (bf16[64,1152]{1,0:T(8,128)(2,1)S(1)}, bf16[64,1152]{1,0:T(8,128)(2,1)S(1)}, u32[]{:S(2)}, u32[]{:S(2)}) collective-permute-start(bf16[64,1152]{1,0:T(8,128)(2,1)S(1)} %get-tuple-element.27), channel_id=1, source_target_pairs={{0,4},{2,6},{4,0},{6,2},{8,12},{10,14},{12,8},{14,10},{1,5},{3,7},... | collective-permute-start | bytes 442376 | tf_op jit(solution)/shard_map/ppermute | solution.py:351
  5.8 1.1 %collective-permute-start.5 = (bf16[64,1152]{1,0:T(8,128)(2,1)S(1)}, bf16[64,1152]{1,0:T(8,128)(2,1)S(1)}, u32[]{:S(2)}, u32[]{:S(2)}) collective-permute-start(bf16[64,1152]{1,0:T(8,128)(2,1)S(1)} %get-tuple-element.28), channel_id=1, source_target_pairs={{0,6},{2,4},{4,2},{6,0},{8,14},{10,12},{12,10},{14,8},{1,7},{3,5},... | collective-permute-start | bytes 442376 | tf_op jit(solution)/shard_map/ppermute | solution.py:351
  6.9 0.2 collective-permute-start.6
  7.2 4.5 %collective-permute-done.10.refs_0_ = bf16[64,1152]{1,0:T(8,128)(2,1)S(1)} collective-permute-done((bf16[64,1152]{1,0:T(8,128)(2,1)S(1)}, bf16[64,1152]{1,0:T(8,128)(2,1)S(1)}, u32[]{:S(2)}, u32[]{:S(2)}) %collective-permute-start.10) | collective-permute-done | bytes 147488 | tf_op jit(solution)/shard_map/ppermute | solution.py:351
  11.7 2.8 %collective-permute-start = (bf16[64,1152]{1,0:T(8,128)(2,1)S(1)}, bf16[64,1152]{1,0:T(8,128)(2,1)S(1)}, u32[]{:S(2)}, u32[]{:S(2)}) collective-permute-start(bf16[64,1152]{1,0:T(8,128)(2,1)S(1)} %get-tuple-element.25), channel_id=1, source_target_pairs={{0,2},{2,0},{4,10},{6,8},{8,6},{10,4},{12,14},{14,12},{1,3},{3,1},... | collective-permute-start | bytes 442376 | tf_op jit(solution)/shard_map/ppermute | solution.py:351
  14.5 0.4 %collective-permute-done.11.refs_1_ = bf16[64,1152]{1,0:T(8,128)(2,1)S(1)} collective-permute-done((bf16[64,1152]{1,0:T(8,128)(2,1)S(1)}, bf16[64,1152]{1,0:T(8,128)(2,1)S(1)}, u32[]{:S(2)}, u32[]{:S(2)}) %collective-permute-start.11) | collective-permute-done | bytes 147488 | tf_op jit(solution)/shard_map/ppermute | solution.py:351
  14.9 2.7 %collective-permute-start.1 = (bf16[64,1152]{1,0:T(8,128)(2,1)S(1)}, bf16[64,1152]{1,0:T(8,128)(2,1)S(1)}, u32[]{:S(2)}, u32[]{:S(2)}) collective-permute-start(bf16[64,1152]{1,0:T(8,128)(2,1)S(1)} %get-tuple-element.26), channel_id=1, source_target_pairs={{0,12},{2,14},{4,8},{6,10},{8,4},{10,6},{12,0},{14,2},{1,13},{3,15... | collective-permute-start | bytes 442376 | tf_op jit(solution)/shard_map/ppermute | solution.py:351
  17.7 1.1 %collective-permute-start.12 = (bf16[64,1152]{1,0:T(8,128)(2,1)S(1)}, bf16[64,1152]{1,0:T(8,128)(2,1)S(1)}, u32[]{:S(2)}, u32[]{:S(2)}) collective-permute-start(bf16[64,1152]{1,0:T(8,128)(2,1)S(1)} %collective-permute-done.10.refs_0_), channel_id=1, source_target_pairs={{0,1},{1,0},{2,3},{3,2},{4,5},{5,4},{6,7},{7,6},{8,9},{9,8},{10,11... | collective-permute-start | bytes 442376 | tf_op jit(solution)/shard_map/ppermute | solution.py:359
  18.8 3.7 %collective-permute-start.13 = (bf16[64,1152]{1,0:T(8,128)(2,1)S(1)}, bf16[64,1152]{1,0:T(8,128)(2,1)S(1)}, u32[]{:S(2)}, u32[]{:S(2)}) collective-permute-start(bf16[64,1152]{1,0:T(8,128)(2,1)S(1)} %collective-permute-done.11.refs_1_), channel_id=1, source_target_pairs={{0,1},{1,0},{2,3},{3,2},{4,5},{5,4},{6,7},{7,6},{8,9},{9,8},{10,11... | collective-permute-start | bytes 442376 | tf_op jit(solution)/shard_map/ppermute | solution.py:359
  22.5 5.4 %collective-permute-done.refs_0_ = bf16[64,1152]{1,0:T(8,128)(2,1)S(1)} collective-permute-done((bf16[64,1152]{1,0:T(8,128)(2,1)S(1)}, bf16[64,1152]{1,0:T(8,128)(2,1)S(1)}, u32[]{:S(2)}, u32[]{:S(2)}) %collective-permute-start) | collective-permute-done | bytes 147488 | tf_op jit(solution)/shard_map/ppermute | solution.py:351
  27.9 0.5 %collective-permute-start.8 = (bf16[64,1152]{1,0:T(8,128)(2,1)S(1)}, bf16[64,1152]{1,0:T(8,128)(2,1)S(1)}, u32[]{:S(2)}, u32[]{:S(2)}) collective-permute-start(bf16[64,1152]{1,0:T(8,128)(2,1)S(1)} %collective-permute-done.5.refs_1_), channel_id=1, source_target_pairs={{0,1},{1,0},{2,3},{3,2},{4,5},{5,4},{6,7},{7,6},{8,9},{9,8},{10,11... | collective-permute-start | bytes 442376 | tf_op jit(solution)/shard_map/ppermute | solution.py:359
  28.4 2.7 %collective-permute-done.1.refs_1_ = bf16[64,1152]{1,0:T(8,128)(2,1)S(1)} collective-permute-done((bf16[64,1152]{1,0:T(8,128)(2,1)S(1)}, bf16[64,1152]{1,0:T(8,128)(2,1)S(1)}, u32[]{:S(2)}, u32[]{:S(2)}) %collective-permute-start.1) | collective-permute-done | bytes 147488 | tf_op jit(solution)/shard_map/ppermute | solution.py:351
  31.1 0.4 %collective-permute-start.9 = (bf16[64,1152]{1,0:T(8,128)(2,1)S(1)}, bf16[64,1152]{1,0:T(8,128)(2,1)S(1)}, u32[]{:S(2)}, u32[]{:S(2)}) collective-permute-start(bf16[64,1152]{1,0:T(8,128)(2,1)S(1)} %collective-permute-done.6.refs_2_), channel_id=1, source_target_pairs={{0,1},{1,0},{2,3},{3,2},{4,5},{5,4},{6,7},{7,6},{8,9},{9,8},{10,11... | collective-permute-start | bytes 442376 | tf_op jit(solution)/shard_map/ppermute | solution.py:359
  31.5 0.1 collective-permute-start.2
  31.6 0.4 %collective-permute-start.3 = (bf16[64,1152]{1,0:T(8,128)(2,1)S(1)}, bf16[64,1152]{1,0:T(8,128)(2,1)S(1)}, u32[]{:S(2)}, u32[]{:S(2)}) collective-permute-start(bf16[64,1152]{1,0:T(8,128)(2,1)S(1)} %collective-permute-done.1.refs_1_), channel_id=1, source_target_pairs={{0,1},{1,0},{2,3},{3,2},{4,5},{5,4},{6,7},{7,6},{8,9},{9,8},{10,11... | collective-permute-start | bytes 442376 | tf_op jit(solution)/shard_map/ppermute | solution.py:359
  32.1 1.3 %spread.1 = (bf16[2,256,640]{2,1,0:T(8,128)(2,1)S(1)}, bf16[2,576,256]{2,1,0:T(8,128)(2,1)S(1)}) custom-call(bf16[4,2,64,576]{3,2,1,0:T(8,128)(2,1)} %q_hbm.1, bf16[2,576,256]{2,1,0:T(8,128)(2,1)} %bitcast.7), custom_call_target="tpu_custom_call" | custom-call | tf_op jit(solution)/shard_map/spread/pallas_call | solution.py:151
  33.4 0.8 %bias.1.bias_ref = f32[2,1280,128]{2,1,0:T(8,128)S(1)} custom-call(s32[16]{0:T(128)} %assign_hbm.3, s32[16]{0:T(128)} %length_hbm.1, s32[2]{0:T(128)} %ctx_hbm.1), custom_call_target="tpu_custom_call" | custom-call | tf_op jit(solution)/shard_map/bias/pallas_call | solution.py:112
  34.2 1.2 %attend.3 = (f32[2,1,256]{2,1,0:T(1,128)S(1)}, f32[2,1,256]{2,1,0:T(1,128)S(1)}, f32[2,256,512]{2,1,0:T(8,128)S(1)}) custom-call(f32[2,1280,128]{2,1,0:T(8,128)S(1)} %bias.1.bias_ref, bf16[2,256,640]{2,1,0:T(8,128)(2,1)S(1)} %get-tuple-element.24.q_ref, bf16[64,1152]{1,0:T(8,128)(2,1)S(1)} %get-tuple-element.32.refs_0_, ...), custom_call_target="tpu_custom_call" | custom-call | flops 150994944 | bytes 983040 | tf_op jit(solution)/shard_map/attend/pallas_call | solution.py:275
  35.4 0.8 %attend.4 = (f32[2,1,256]{2,1,0:T(1,128)S(1)}, f32[2,1,256]{2,1,0:T(1,128)S(1)}, f32[2,256,512]{2,1,0:T(8,128)S(1)}) custom-call(f32[2,1280,128]{2,1,0:T(8,128)S(1)} %bias.1.bias_ref, bf16[2,256,640]{2,1,0:T(8,128)(2,1)S(1)} %get-tuple-element.24.q_ref, bf16[64,1152]{1,0:T(8,128)(2,1)S(1)} %collective-permute-done.10.refs_0_, ...), custom_call_target="tpu_custom_call" | custom-call | flops 301989888 | bytes 1310720 | tf_op jit(solution)/shard_map/attend/pallas_call | solution.py:275
  36.3 1.1 %attend.5 = (f32[2,1,256]{2,1,0:T(1,128)S(1)}, f32[2,1,256]{2,1,0:T(1,128)S(1)}, f32[2,256,512]{2,1,0:T(8,128)S(1)}) custom-call(f32[2,1280,128]{2,1,0:T(8,128)S(1)} %bias.1.bias_ref, bf16[2,256,640]{2,1,0:T(8,128)(2,1)S(1)} %get-tuple-element.24.q_ref, bf16[64,1152]{1,0:T(8,128)(2,1)S(1)} %collective-permute-done.4.refs_0_, ...), custom_call_target="tpu_custom_call" | custom-call | flops 452984832 | bytes 1638400 | tf_op jit(solution)/shard_map/attend/pallas_call | solution.py:275
  37.4 1.6 %attend_last.1 = bf16[4,2,64,512]{3,2,1,0:T(8,128)(2,1)} custom-call(f32[2,1280,128]{2,1,0:T(8,128)S(1)} %bias.1.bias_ref, bf16[2,256,640]{2,1,0:T(8,128)(2,1)S(1)} %get-tuple-element.24.q_ref, bf16[64,1152]{1,0:T(8,128)(2,1)S(1)} %collective-permute-done.refs_0_, bf16[64,1152]{1,0:T(8,128)(2,1)S(1)} %collective-permute-done.1.refs_1_, ...), custom_call_target="tpu_custom_call" | custom-call | flops 301989888 | bytes 1310720 | tf_op jit(solution)/shard_map/attend_last/pallas_call | solution.py:275
  (16 shorter events, 0.1 us)
Async XLA Ops:
  0.0 32.1 %copy-start = (bf16[4,2,576]{2,1,0:T(2,128)(2,1)S(1)}, bf16[4,2,576]{2,1,0:T(2,128)(2,1)}, u32[]{:S(2)}) copy-start(bf16[4,2,576]{2,1,0:T(2,128)(2,1)} %param.10) | copy-start | bytes 27652
  1.5 5.5 %collective-permute-start.14 = (bf16[64,1152]{1,0:T(8,128)(2,1)S(1)}, bf16[64,1152]{1,0:T(8,128)(2,1)S(1)}, u32[]{:S(2)}, u32[]{:S(2)}) collective-permute-start(bf16[64,1152]{1,0:T(8,128)(2,1)S(1)} %get-tuple-element.32.refs_0_), channel_id=1, source_target_pairs={{0,1},{1,0},{2,3},{3,2},{4,5},{5,4},{6,7},{7,6},{8,9},{9,8},{10,11... | collective-permute-start | bytes 442376 | tf_op jit(solution)/shard_map/ppermute | solution.py:359
  2.2 9.5 %collective-permute-start.10 = (bf16[64,1152]{1,0:T(8,128)(2,1)S(1)}, bf16[64,1152]{1,0:T(8,128)(2,1)S(1)}, u32[]{:S(2)}, u32[]{:S(2)}) collective-permute-start(bf16[64,1152]{1,0:T(8,128)(2,1)S(1)} %get-tuple-element.30), channel_id=1, source_target_pairs={{0,8},{2,10},{4,12},{6,14},{8,0},{10,2},{12,4},{14,6},{1,9},{3,11}... | collective-permute-start | bytes 442376 | tf_op jit(solution)/shard_map/ppermute | solution.py:351
  2.3 12.7 %collective-permute-start.11 = (bf16[64,1152]{1,0:T(8,128)(2,1)S(1)}, bf16[64,1152]{1,0:T(8,128)(2,1)S(1)}, u32[]{:S(2)}, u32[]{:S(2)}) collective-permute-start(bf16[64,1152]{1,0:T(8,128)(2,1)S(1)} %get-tuple-element.31), channel_id=1, source_target_pairs={{0,10},{2,8},{4,14},{6,12},{8,2},{10,0},{12,6},{14,4},{1,11},{3,9}... | collective-permute-start | bytes 442376 | tf_op jit(solution)/shard_map/ppermute | solution.py:351
  4.5 13.2 %collective-permute-start.4 = (bf16[64,1152]{1,0:T(8,128)(2,1)S(1)}, bf16[64,1152]{1,0:T(8,128)(2,1)S(1)}, u32[]{:S(2)}, u32[]{:S(2)}) collective-permute-start(bf16[64,1152]{1,0:T(8,128)(2,1)S(1)} %get-tuple-element.27), channel_id=1, source_target_pairs={{0,4},{2,6},{4,0},{6,2},{8,12},{10,14},{12,8},{14,10},{1,5},{3,7},... | collective-permute-start | bytes 442376 | tf_op jit(solution)/shard_map/ppermute | solution.py:351
  5.8 13.0 %collective-permute-start.5 = (bf16[64,1152]{1,0:T(8,128)(2,1)S(1)}, bf16[64,1152]{1,0:T(8,128)(2,1)S(1)}, u32[]{:S(2)}, u32[]{:S(2)}) collective-permute-start(bf16[64,1152]{1,0:T(8,128)(2,1)S(1)} %get-tuple-element.28), channel_id=1, source_target_pairs={{0,6},{2,4},{4,2},{6,0},{8,14},{10,12},{12,10},{14,8},{1,7},{3,5},... | collective-permute-start | bytes 442376 | tf_op jit(solution)/shard_map/ppermute | solution.py:351
  6.9 15.5 %collective-permute-start.6 = (bf16[64,1152]{1,0:T(8,128)(2,1)S(1)}, bf16[64,1152]{1,0:T(8,128)(2,1)S(1)}, u32[]{:S(2)}, u32[]{:S(2)}) collective-permute-start(bf16[64,1152]{1,0:T(8,128)(2,1)S(1)} %get-tuple-element.29), channel_id=1, source_target_pairs={{0,14},{2,12},{4,6},{6,4},{8,10},{10,8},{12,2},{14,0},{1,15},{3,13... | collective-permute-start | bytes 442376 | tf_op jit(solution)/shard_map/ppermute | solution.py:351
  11.7 16.2 %collective-permute-start = (bf16[64,1152]{1,0:T(8,128)(2,1)S(1)}, bf16[64,1152]{1,0:T(8,128)(2,1)S(1)}, u32[]{:S(2)}, u32[]{:S(2)}) collective-permute-start(bf16[64,1152]{1,0:T(8,128)(2,1)S(1)} %get-tuple-element.25), channel_id=1, source_target_pairs={{0,2},{2,0},{4,10},{6,8},{8,6},{10,4},{12,14},{14,12},{1,3},{3,1},... | collective-permute-start | bytes 442376 | tf_op jit(solution)/shard_map/ppermute | solution.py:351
  14.9 16.2 %collective-permute-start.1 = (bf16[64,1152]{1,0:T(8,128)(2,1)S(1)}, bf16[64,1152]{1,0:T(8,128)(2,1)S(1)}, u32[]{:S(2)}, u32[]{:S(2)}) collective-permute-start(bf16[64,1152]{1,0:T(8,128)(2,1)S(1)} %get-tuple-element.26), channel_id=1, source_target_pairs={{0,12},{2,14},{4,8},{6,10},{8,4},{10,6},{12,0},{14,2},{1,13},{3,15... | collective-permute-start | bytes 442376 | tf_op jit(solution)/shard_map/ppermute | solution.py:351
  17.7 13.9 %collective-permute-start.12 = (bf16[64,1152]{1,0:T(8,128)(2,1)S(1)}, bf16[64,1152]{1,0:T(8,128)(2,1)S(1)}, u32[]{:S(2)}, u32[]{:S(2)}) collective-permute-start(bf16[64,1152]{1,0:T(8,128)(2,1)S(1)} %collective-permute-done.10.refs_0_), channel_id=1, source_target_pairs={{0,1},{1,0},{2,3},{3,2},{4,5},{5,4},{6,7},{7,6},{8,9},{9,8},{10,11... | collective-permute-start | bytes 442376 | tf_op jit(solution)/shard_map/ppermute | solution.py:359
  18.8 12.8 %collective-permute-start.13 = (bf16[64,1152]{1,0:T(8,128)(2,1)S(1)}, bf16[64,1152]{1,0:T(8,128)(2,1)S(1)}, u32[]{:S(2)}, u32[]{:S(2)}) collective-permute-start(bf16[64,1152]{1,0:T(8,128)(2,1)S(1)} %collective-permute-done.11.refs_1_), channel_id=1, source_target_pairs={{0,1},{1,0},{2,3},{3,2},{4,5},{5,4},{6,7},{7,6},{8,9},{9,8},{10,11... | collective-permute-start | bytes 442376 | tf_op jit(solution)/shard_map/ppermute | solution.py:359
  22.5 13.8 %collective-permute-start.7 = (bf16[64,1152]{1,0:T(8,128)(2,1)S(1)}, bf16[64,1152]{1,0:T(8,128)(2,1)S(1)}, u32[]{:S(2)}, u32[]{:S(2)}) collective-permute-start(bf16[64,1152]{1,0:T(8,128)(2,1)S(1)} %collective-permute-done.4.refs_0_), channel_id=1, source_target_pairs={{0,1},{1,0},{2,3},{3,2},{4,5},{5,4},{6,7},{7,6},{8,9},{9,8},{10,11... | collective-permute-start | bytes 442376 | tf_op jit(solution)/shard_map/ppermute | solution.py:359
  27.9 8.4 %collective-permute-start.8 = (bf16[64,1152]{1,0:T(8,128)(2,1)S(1)}, bf16[64,1152]{1,0:T(8,128)(2,1)S(1)}, u32[]{:S(2)}, u32[]{:S(2)}) collective-permute-start(bf16[64,1152]{1,0:T(8,128)(2,1)S(1)} %collective-permute-done.5.refs_1_), channel_id=1, source_target_pairs={{0,1},{1,0},{2,3},{3,2},{4,5},{5,4},{6,7},{7,6},{8,9},{9,8},{10,11... | collective-permute-start | bytes 442376 | tf_op jit(solution)/shard_map/ppermute | solution.py:359
  31.1 5.2 %collective-permute-start.9 = (bf16[64,1152]{1,0:T(8,128)(2,1)S(1)}, bf16[64,1152]{1,0:T(8,128)(2,1)S(1)}, u32[]{:S(2)}, u32[]{:S(2)}) collective-permute-start(bf16[64,1152]{1,0:T(8,128)(2,1)S(1)} %collective-permute-done.6.refs_2_), channel_id=1, source_target_pairs={{0,1},{1,0},{2,3},{3,2},{4,5},{5,4},{6,7},{7,6},{8,9},{9,8},{10,11... | collective-permute-start | bytes 442376 | tf_op jit(solution)/shard_map/ppermute | solution.py:359
  31.5 5.8 %collective-permute-start.2 = (bf16[64,1152]{1,0:T(8,128)(2,1)S(1)}, bf16[64,1152]{1,0:T(8,128)(2,1)S(1)}, u32[]{:S(2)}, u32[]{:S(2)}) collective-permute-start(bf16[64,1152]{1,0:T(8,128)(2,1)S(1)} %collective-permute-done.refs_0_), channel_id=1, source_target_pairs={{0,1},{1,0},{2,3},{3,2},{4,5},{5,4},{6,7},{7,6},{8,9},{9,8},{10,11... | collective-permute-start | bytes 442376 | tf_op jit(solution)/shard_map/ppermute | solution.py:359
  31.6 5.8 %collective-permute-start.3 = (bf16[64,1152]{1,0:T(8,128)(2,1)S(1)}, bf16[64,1152]{1,0:T(8,128)(2,1)S(1)}, u32[]{:S(2)}, u32[]{:S(2)}) collective-permute-start(bf16[64,1152]{1,0:T(8,128)(2,1)S(1)} %collective-permute-done.1.refs_1_), channel_id=1, source_target_pairs={{0,1},{1,0},{2,3},{3,2},{4,5},{5,4},{6,7},{7,6},{8,9},{9,8},{10,11... | collective-permute-start | bytes 442376 | tf_op jit(solution)/shard_map/ppermute | solution.py:359
where the time goes:
time: 39.1 us; the launch traced here: 39 us
  starting transfers between devices  17.5 us (45%)
  waiting for transfers between devices  13.1 us (34%)
  Pallas kernels  8.26 us (21%)
    ppermute x7, waiting for transfers between devices, shards(): mine[offset] = lax.ppermute(packed[offset], 'row', pairs)  13.1 us
    ppermute x7, starting transfers between devices, shards(): mine[offset] = lax.ppermute(packed[offset], 'row', pairs)  10.5 us
    ppermute x8, starting transfers between devices, shards(): theirs[offset] = lax.ppermute(mine[offset], 'tp', [(0, 1), (1, 0)])  6.98 us
    pallas_call x4, Pallas kernels, attend(): pl.pallas_call(functools.partial(attend_kernel, offsets, heads, first, la...  4.68 us
    pallas_call x1, Pallas kernels, pack(): pl.pallas_call(functools.partial(pack_kernel, order, rows_here), out_shap...  1.46 us
    pallas_call x1, Pallas kernels, spread_queries(): pl.pallas_call(spread_kernel, out_shape=[jax.ShapeDtypeStruct((rows, step...  1.28 us
    pallas_call x1, Pallas kernels, make_bias(): pl.pallas_call(functools.partial(bias_kernel, piece), out_shape=jax.Shape...  0.84 us
  transfers between devices with their start and end apart: 15, of which 4 were waited for; matrix products, arithmetic and copies ran while one was open for 0% of the time, Pallas kernels for 13%

commit v1 on v0

--- a/solution.py
+++ b/solution.py
@@ -235,20 +235,26 @@
         weights.append([part.astype(q_ref.dtype) for part in parts])
     copies = []
     for r in every:
+        if last:
+            shrunk = column(shrinks[r])
+            for part in range(tall // LANES):
+                here = slice(part * LANES, (part + 1) * LANES)
+                acc = dot(weights[r][0][:, here], value[r], by_key)
+                acc += shrunk[here] * acc_in[r, here]
+                steps = slice(part * LANES // heads, (part + 1) * LANES // heads)
+                done = acc.astype(out_ref.dtype)
+                stage_ref[r, steps] = done.reshape(LANES // heads, heads, KV_RANK)
+                source, target = stage_ref.at[r, steps], out_ref.at[steps, r]
+                copies.append(pltpu.make_async_copy(source, target, sems.at[r, part]))
+                copies[-1].start()
+            continue
         acc = dot(weights[r][0], value[r], by_key)
         if first:
             acc += dot(weights[r][1].T, cache_ref[r, :KV_RANK], by_width)
             acc += dot(weights[r][2], new_ref[r, :, :KV_RANK], by_key)
         else:
             acc += column(shrinks[r]) * acc_in[r]
-        if last:
-            stage_ref[r] = acc.astype(out_ref.dtype).reshape(tall // heads, heads, KV_RANK)
-            copies.append(
-                pltpu.make_async_copy(stage_ref.at[r], out_ref.at[:, r], sems.at[r])
-            )
-            copies[r].start()
-        else:
-            acc_out[r] = acc
+        acc_out[r] = acc
     for copy in copies:
         copy.wait()
 
@@ -270,7 +276,7 @@
     if last:
         scratch = [
             pltpu.VMEM((rows, steps, heads, KV_RANK), wide.dtype),
-            pltpu.SemaphoreType.DMA((rows,)),
+            pltpu.SemaphoreType.DMA((rows, tall // LANES)),
         ]
     return pl.pallas_call(
         functools.partial(attend_kernel, offsets, heads, first, last),

time: 39.1 us -> 39.1 us (level)
  no operation moved by 1% of the time
where the time goes in v1:
time: 39.1 us; the launch traced here: 38.9 us
  starting transfers between devices  17.5 us (45%)
  waiting for transfers between devices  13.1 us (34%)
  Pallas kernels  8.24 us (21%)
    ppermute x7, waiting for transfers between devices, shards(): mine[offset] = lax.ppermute(packed[offset], 'row', pairs)  13.1 us
    ppermute x7, starting transfers between devices, shards(): mine[offset] = lax.ppermute(packed[offset], 'row', pairs)  10.5 us
    ppermute x8, starting transfers between devices, shards(): theirs[offset] = lax.ppermute(mine[offset], 'tp', [(0, 1), (1, 0)])  6.98 us
    pallas_call x4, Pallas kernels, attend(): pl.pallas_call(functools.partial(attend_kernel, offsets, heads, first, la...  4.66 us
    pallas_call x1, Pallas kernels, pack(): pl.pallas_call(functools.partial(pack_kernel, order, rows_here), out_shap...  1.46 us
    pallas_call x1, Pallas kernels, spread_queries(): pl.pallas_call(spread_kernel, out_shape=[jax.ShapeDtypeStruct((rows, step...  1.28 us
    pallas_call x1, Pallas kernels, make_bias(): pl.pallas_call(functools.partial(bias_kernel, piece), out_shape=jax.Shape...  0.84 us
  transfers between devices with their start and end apart: 15, of which 4 were waited for; matrix products, arithmetic and copies ran while one was open for 0% of the time, Pallas kernels for 13%

profile of v1, /device:TPU:21, one launch (start us, length us, event | category | flops | bytes accessed | tf_op | source)
XLA Modules:
  0.0 38.9 jit_solution(8211421163064539430)
XLA Ops:
  0.0 1.5 %pack.1 = (bf16[64,1152]{1,0:T(8,128)(2,1)S(1)}, bf16[64,1152]{1,0:T(8,128)(2,1)S(1)}, bf16[64,1152]{1,0:T(8,128)(2,1)S(1)}, bf16[64,1152]{1,0:T(8,128)(2,1)S(1)...) custom-call(s32[16]{0:T(128)} %assign_hbm.3, ...), custom_call_target="tpu_custom_call" | custom-call | tf_op jit(solution)/shard_map/pack/pallas_call | solution.py:76
  1.5 0.7 %collective-permute-start.14 = (bf16[64,1152]{1,0:T(8,128)(2,1)S(1)}, bf16[64,1152]{1,0:T(8,128)(2,1)S(1)}, u32[]{:S(2)}, u32[]{:S(2)}) collective-permute-start(bf16[64,1152]{1,0:T(8,128)(2,1)S(1)} %get-tuple-element.32.refs_0_), channel_id=1, source_target_pairs={{0,1},{1,0},{2,3},{3,2},{4,5},{5,4},{6,7},{7,6},{8,9},{9,8},{10,11... | collective-permute-start | bytes 442376 | tf_op jit(solution)/shard_map/ppermute | solution.py:365
  2.3 2.3 %collective-permute-start.11 = (bf16[64,1152]{1,0:T(8,128)(2,1)S(1)}, bf16[64,1152]{1,0:T(8,128)(2,1)S(1)}, u32[]{:S(2)}, u32[]{:S(2)}) collective-permute-start(bf16[64,1152]{1,0:T(8,128)(2,1)S(1)} %get-tuple-element.31), channel_id=1, source_target_pairs={{0,10},{2,8},{4,14},{6,12},{8,2},{10,0},{12,6},{14,4},{1,11},{3,9}... | collective-permute-start | bytes 442376 | tf_op jit(solution)/shard_map/ppermute | solution.py:357
  4.5 1.3 %collective-permute-start.4 = (bf16[64,1152]{1,0:T(8,128)(2,1)S(1)}, bf16[64,1152]{1,0:T(8,128)(2,1)S(1)}, u32[]{:S(2)}, u32[]{:S(2)}) collective-permute-start(bf16[64,1152]{1,0:T(8,128)(2,1)S(1)} %get-tuple-element.27), channel_id=1, source_target_pairs={{0,4},{2,6},{4,0},{6,2},{8,12},{10,14},{12,8},{14,10},{1,5},{3,7},... | collective-permute-start | bytes 442376 | tf_op jit(solution)/shard_map/ppermute | solution.py:357
  5.8 1.1 %collective-permute-start.5 = (bf16[64,1152]{1,0:T(8,128)(2,1)S(1)}, bf16[64,1152]{1,0:T(8,128)(2,1)S(1)}, u32[]{:S(2)}, u32[]{:S(2)}) collective-permute-start(bf16[64,1152]{1,0:T(8,128)(2,1)S(1)} %get-tuple-element.28), channel_id=1, source_target_pairs={{0,6},{2,4},{4,2},{6,0},{8,14},{10,12},{12,10},{14,8},{1,7},{3,5},... | collective-permute-start | bytes 442376 | tf_op jit(solution)/shard_map/ppermute | solution.py:357
  6.9 0.2 collective-permute-start.6
  7.2 4.5 %collective-permute-done.10.refs_0_ = bf16[64,1152]{1,0:T(8,128)(2,1)S(1)} collective-permute-done((bf16[64,1152]{1,0:T(8,128)(2,1)S(1)}, bf16[64,1152]{1,0:T(8,128)(2,1)S(1)}, u32[]{:S(2)}, u32[]{:S(2)}) %collective-permute-start.10) | collective-permute-done | bytes 147488 | tf_op jit(solution)/shard_map/ppermute | solution.py:357
  11.7 2.8 %collective-permute-start = (bf16[64,1152]{1,0:T(8,128)(2,1)S(1)}, bf16[64,1152]{1,0:T(8,128)(2,1)S(1)}, u32[]{:S(2)}, u32[]{:S(2)}) collective-permute-start(bf16[64,1152]{1,0:T(8,128)(2,1)S(1)} %get-tuple-element.25), channel_id=1, source_target_pairs={{0,2},{2,0},{4,10},{6,8},{8,6},{10,4},{12,14},{14,12},{1,3},{3,1},... | collective-permute-start | bytes 442376 | tf_op jit(solution)/shard_map/ppermute | solution.py:357
  14.5 0.4 %collective-permute-done.11.refs_1_ = bf16[64,1152]{1,0:T(8,128)(2,1)S(1)} collective-permute-done((bf16[64,1152]{1,0:T(8,128)(2,1)S(1)}, bf16[64,1152]{1,0:T(8,128)(2,1)S(1)}, u32[]{:S(2)}, u32[]{:S(2)}) %collective-permute-start.11) | collective-permute-done | bytes 147488 | tf_op jit(solution)/shard_map/ppermute | solution.py:357
  14.9 2.7 %collective-permute-start.1 = (bf16[64,1152]{1,0:T(8,128)(2,1)S(1)}, bf16[64,1152]{1,0:T(8,128)(2,1)S(1)}, u32[]{:S(2)}, u32[]{:S(2)}) collective-permute-start(bf16[64,1152]{1,0:T(8,128)(2,1)S(1)} %get-tuple-element.26), channel_id=1, source_target_pairs={{0,12},{2,14},{4,8},{6,10},{8,4},{10,6},{12,0},{14,2},{1,13},{3,15... | collective-permute-start | bytes 442376 | tf_op jit(solution)/shard_map/ppermute | solution.py:357
  17.7 1.1 %collective-permute-start.12 = (bf16[64,1152]{1,0:T(8,128)(2,1)S(1)}, bf16[64,1152]{1,0:T(8,128)(2,1)S(1)}, u32[]{:S(2)}, u32[]{:S(2)}) collective-permute-start(bf16[64,1152]{1,0:T(8,128)(2,1)S(1)} %collective-permute-done.10.refs_0_), channel_id=1, source_target_pairs={{0,1},{1,0},{2,3},{3,2},{4,5},{5,4},{6,7},{7,6},{8,9},{9,8},{10,11... | collective-permute-start | bytes 442376 | tf_op jit(solution)/shard_map/ppermute | solution.py:365
  18.8 3.7 %collective-permute-start.13 = (bf16[64,1152]{1,0:T(8,128)(2,1)S(1)}, bf16[64,1152]{1,0:T(8,128)(2,1)S(1)}, u32[]{:S(2)}, u32[]{:S(2)}) collective-permute-start(bf16[64,1152]{1,0:T(8,128)(2,1)S(1)} %collective-permute-done.11.refs_1_), channel_id=1, source_target_pairs={{0,1},{1,0},{2,3},{3,2},{4,5},{5,4},{6,7},{7,6},{8,9},{9,8},{10,11... | collective-permute-start | bytes 442376 | tf_op jit(solution)/shard_map/ppermute | solution.py:365
  22.5 5.4 %collective-permute-done.refs_0_ = bf16[64,1152]{1,0:T(8,128)(2,1)S(1)} collective-permute-done((bf16[64,1152]{1,0:T(8,128)(2,1)S(1)}, bf16[64,1152]{1,0:T(8,128)(2,1)S(1)}, u32[]{:S(2)}, u32[]{:S(2)}) %collective-permute-start) | collective-permute-done | bytes 147488 | tf_op jit(solution)/shard_map/ppermute | solution.py:357
  27.9 0.5 %collective-permute-start.8 = (bf16[64,1152]{1,0:T(8,128)(2,1)S(1)}, bf16[64,1152]{1,0:T(8,128)(2,1)S(1)}, u32[]{:S(2)}, u32[]{:S(2)}) collective-permute-start(bf16[64,1152]{1,0:T(8,128)(2,1)S(1)} %collective-permute-done.5.refs_1_), channel_id=1, source_target_pairs={{0,1},{1,0},{2,3},{3,2},{4,5},{5,4},{6,7},{7,6},{8,9},{9,8},{10,11... | collective-permute-start | bytes 442376 | tf_op jit(solution)/shard_map/ppermute | solution.py:365
  28.4 2.7 %collective-permute-done.1.refs_1_ = bf16[64,1152]{1,0:T(8,128)(2,1)S(1)} collective-permute-done((bf16[64,1152]{1,0:T(8,128)(2,1)S(1)}, bf16[64,1152]{1,0:T(8,128)(2,1)S(1)}, u32[]{:S(2)}, u32[]{:S(2)}) %collective-permute-start.1) | collective-permute-done | bytes 147488 | tf_op jit(solution)/shard_map/ppermute | solution.py:357
  31.1 0.4 %collective-permute-start.9 = (bf16[64,1152]{1,0:T(8,128)(2,1)S(1)}, bf16[64,1152]{1,0:T(8,128)(2,1)S(1)}, u32[]{:S(2)}, u32[]{:S(2)}) collective-permute-start(bf16[64,1152]{1,0:T(8,128)(2,1)S(1)} %collective-permute-done.6.refs_2_), channel_id=1, source_target_pairs={{0,1},{1,0},{2,3},{3,2},{4,5},{5,4},{6,7},{7,6},{8,9},{9,8},{10,11... | collective-permute-start | bytes 442376 | tf_op jit(solution)/shard_map/ppermute | solution.py:365
  31.5 0.1 collective-permute-start.2
  31.6 0.4 %collective-permute-start.3 = (bf16[64,1152]{1,0:T(8,128)(2,1)S(1)}, bf16[64,1152]{1,0:T(8,128)(2,1)S(1)}, u32[]{:S(2)}, u32[]{:S(2)}) collective-permute-start(bf16[64,1152]{1,0:T(8,128)(2,1)S(1)} %collective-permute-done.1.refs_1_), channel_id=1, source_target_pairs={{0,1},{1,0},{2,3},{3,2},{4,5},{5,4},{6,7},{7,6},{8,9},{9,8},{10,11... | collective-permute-start | bytes 442376 | tf_op jit(solution)/shard_map/ppermute | solution.py:365
  32.1 1.3 %spread.1 = (bf16[2,256,640]{2,1,0:T(8,128)(2,1)S(1)}, bf16[2,576,256]{2,1,0:T(8,128)(2,1)S(1)}) custom-call(bf16[4,2,64,576]{3,2,1,0:T(8,128)(2,1)} %q_hbm.1, bf16[2,576,256]{2,1,0:T(8,128)(2,1)} %bitcast.7), custom_call_target="tpu_custom_call" | custom-call | tf_op jit(solution)/shard_map/spread/pallas_call | solution.py:151
  33.4 0.8 %bias.1.bias_ref = f32[2,1280,128]{2,1,0:T(8,128)S(1)} custom-call(s32[16]{0:T(128)} %assign_hbm.3, s32[16]{0:T(128)} %length_hbm.1, s32[2]{0:T(128)} %ctx_hbm.1), custom_call_target="tpu_custom_call" | custom-call | tf_op jit(solution)/shard_map/bias/pallas_call | solution.py:112
  34.2 1.2 %attend.3 = (f32[2,1,256]{2,1,0:T(1,128)S(1)}, f32[2,1,256]{2,1,0:T(1,128)S(1)}, f32[2,256,512]{2,1,0:T(8,128)S(1)}) custom-call(f32[2,1280,128]{2,1,0:T(8,128)S(1)} %bias.1.bias_ref, bf16[2,256,640]{2,1,0:T(8,128)(2,1)S(1)} %get-tuple-element.24.q_ref, bf16[64,1152]{1,0:T(8,128)(2,1)S(1)} %get-tuple-element.32.refs_0_, ...), custom_call_target="tpu_custom_call" | custom-call | flops 150994944 | bytes 983040 | tf_op jit(solution)/shard_map/attend/pallas_call | solution.py:281
  35.4 0.8 %attend.4 = (f32[2,1,256]{2,1,0:T(1,128)S(1)}, f32[2,1,256]{2,1,0:T(1,128)S(1)}, f32[2,256,512]{2,1,0:T(8,128)S(1)}) custom-call(f32[2,1280,128]{2,1,0:T(8,128)S(1)} %bias.1.bias_ref, bf16[2,256,640]{2,1,0:T(8,128)(2,1)S(1)} %get-tuple-element.24.q_ref, bf16[64,1152]{1,0:T(8,128)(2,1)S(1)} %collective-permute-done.10.refs_0_, ...), custom_call_target="tpu_custom_call" | custom-call | flops 301989888 | bytes 1310720 | tf_op jit(solution)/shard_map/attend/pallas_call | solution.py:281
  36.3 1.1 %attend.5 = (f32[2,1,256]{2,1,0:T(1,128)S(1)}, f32[2,1,256]{2,1,0:T(1,128)S(1)}, f32[2,256,512]{2,1,0:T(8,128)S(1)}) custom-call(f32[2,1280,128]{2,1,0:T(8,128)S(1)} %bias.1.bias_ref, bf16[2,256,640]{2,1,0:T(8,128)(2,1)S(1)} %get-tuple-element.24.q_ref, bf16[64,1152]{1,0:T(8,128)(2,1)S(1)} %collective-permute-done.4.refs_0_, ...), custom_call_target="tpu_custom_call" | custom-call | flops 452984832 | bytes 1638400 | tf_op jit(solution)/shard_map/attend/pallas_call | solution.py:281
  37.4 1.5 %attend_last.1 = bf16[4,2,64,512]{3,2,1,0:T(8,128)(2,1)} custom-call(f32[2,1280,128]{2,1,0:T(8,128)S(1)} %bias.1.bias_ref, bf16[2,256,640]{2,1,0:T(8,128)(2,1)S(1)} %get-tuple-element.24.q_ref, bf16[64,1152]{1,0:T(8,128)(2,1)S(1)} %collective-permute-done.refs_0_, bf16[64,1152]{1,0:T(8,128)(2,1)S(1)} %collective-permute-done.1.refs_1_, ...), custom_call_target="tpu_custom_call" | custom-call | flops 301989888 | bytes 1310720 | tf_op jit(solution)/shard_map/attend_last/pallas_call | solution.py:281
  (16 shorter events, 0.1 us)
Async XLA Ops:
  0.0 32.1 %copy-start = (bf16[4,2,576]{2,1,0:T(2,128)(2,1)S(1)}, bf16[4,2,576]{2,1,0:T(2,128)(2,1)}, u32[]{:S(2)}) copy-start(bf16[4,2,576]{2,1,0:T(2,128)(2,1)} %param.10) | copy-start | bytes 27652
  1.5 5.5 %collective-permute-start.14 = (bf16[64,1152]{1,0:T(8,128)(2,1)S(1)}, bf16[64,1152]{1,0:T(8,128)(2,1)S(1)}, u32[]{:S(2)}, u32[]{:S(2)}) collective-permute-start(bf16[64,1152]{1,0:T(8,128)(2,1)S(1)} %get-tuple-element.32.refs_0_), channel_id=1, source_target_pairs={{0,1},{1,0},{2,3},{3,2},{4,5},{5,4},{6,7},{7,6},{8,9},{9,8},{10,11... | collective-permute-start | bytes 442376 | tf_op jit(solution)/shard_map/ppermute | solution.py:365
  2.2 9.5 %collective-permute-start.10 = (bf16[64,1152]{1,0:T(8,128)(2,1)S(1)}, bf16[64,1152]{1,0:T(8,128)(2,1)S(1)}, u32[]{:S(2)}, u32[]{:S(2)}) collective-permute-start(bf16[64,1152]{1,0:T(8,128)(2,1)S(1)} %get-tuple-element.30), channel_id=1, source_target_pairs={{0,8},{2,10},{4,12},{6,14},{8,0},{10,2},{12,4},{14,6},{1,9},{3,11}... | collective-permute-start | bytes 442376 | tf_op jit(solution)/shard_map/ppermute | solution.py:357
  2.3 12.7 %collective-permute-start.11 = (bf16[64,1152]{1,0:T(8,128)(2,1)S(1)}, bf16[64,1152]{1,0:T(8,128)(2,1)S(1)}, u32[]{:S(2)}, u32[]{:S(2)}) collective-permute-start(bf16[64,1152]{1,0:T(8,128)(2,1)S(1)} %get-tuple-element.31), channel_id=1, source_target_pairs={{0,10},{2,8},{4,14},{6,12},{8,2},{10,0},{12,6},{14,4},{1,11},{3,9}... | collective-permute-start | bytes 442376 | tf_op jit(solution)/shard_map/ppermute | solution.py:357
  4.5 13.2 %collective-permute-start.4 = (bf16[64,1152]{1,0:T(8,128)(2,1)S(1)}, bf16[64,1152]{1,0:T(8,128)(2,1)S(1)}, u32[]{:S(2)}, u32[]{:S(2)}) collective-permute-start(bf16[64,1152]{1,0:T(8,128)(2,1)S(1)} %get-tuple-element.27), channel_id=1, source_target_pairs={{0,4},{2,6},{4,0},{6,2},{8,12},{10,14},{12,8},{14,10},{1,5},{3,7},... | collective-permute-start | bytes 442376 | tf_op jit(solution)/shard_map/ppermute | solution.py:357
  5.8 13.0 %collective-permute-start.5 = (bf16[64,1152]{1,0:T(8,128)(2,1)S(1)}, bf16[64,1152]{1,0:T(8,128)(2,1)S(1)}, u32[]{:S(2)}, u32[]{:S(2)}) collective-permute-start(bf16[64,1152]{1,0:T(8,128)(2,1)S(1)} %get-tuple-element.28), channel_id=1, source_target_pairs={{0,6},{2,4},{4,2},{6,0},{8,14},{10,12},{12,10},{14,8},{1,7},{3,5},... | collective-permute-start | bytes 442376 | tf_op jit(solution)/shard_map/ppermute | solution.py:357
  6.9 15.5 %collective-permute-start.6 = (bf16[64,1152]{1,0:T(8,128)(2,1)S(1)}, bf16[64,1152]{1,0:T(8,128)(2,1)S(1)}, u32[]{:S(2)}, u32[]{:S(2)}) collective-permute-start(bf16[64,1152]{1,0:T(8,128)(2,1)S(1)} %get-tuple-element.29), channel_id=1, source_target_pairs={{0,14},{2,12},{4,6},{6,4},{8,10},{10,8},{12,2},{14,0},{1,15},{3,13... | collective-permute-start | bytes 442376 | tf_op jit(solution)/shard_map/ppermute | solution.py:357
  11.7 16.2 %collective-permute-start = (bf16[64,1152]{1,0:T(8,128)(2,1)S(1)}, bf16[64,1152]{1,0:T(8,128)(2,1)S(1)}, u32[]{:S(2)}, u32[]{:S(2)}) collective-permute-start(bf16[64,1152]{1,0:T(8,128)(2,1)S(1)} %get-tuple-element.25), channel_id=1, source_target_pairs={{0,2},{2,0},{4,10},{6,8},{8,6},{10,4},{12,14},{14,12},{1,3},{3,1},... | collective-permute-start | bytes 442376 | tf_op jit(solution)/shard_map/ppermute | solution.py:357
  14.9 16.2 %collective-permute-start.1 = (bf16[64,1152]{1,0:T(8,128)(2,1)S(1)}, bf16[64,1152]{1,0:T(8,128)(2,1)S(1)}, u32[]{:S(2)}, u32[]{:S(2)}) collective-permute-start(bf16[64,1152]{1,0:T(8,128)(2,1)S(1)} %get-tuple-element.26), channel_id=1, source_target_pairs={{0,12},{2,14},{4,8},{6,10},{8,4},{10,6},{12,0},{14,2},{1,13},{3,15... | collective-permute-start | bytes 442376 | tf_op jit(solution)/shard_map/ppermute | solution.py:357
  17.7 13.9 %collective-permute-start.12 = (bf16[64,1152]{1,0:T(8,128)(2,1)S(1)}, bf16[64,1152]{1,0:T(8,128)(2,1)S(1)}, u32[]{:S(2)}, u32[]{:S(2)}) collective-permute-start(bf16[64,1152]{1,0:T(8,128)(2,1)S(1)} %collective-permute-done.10.refs_0_), channel_id=1, source_target_pairs={{0,1},{1,0},{2,3},{3,2},{4,5},{5,4},{6,7},{7,6},{8,9},{9,8},{10,11... | collective-permute-start | bytes 442376 | tf_op jit(solution)/shard_map/ppermute | solution.py:365
  18.8 12.8 %collective-permute-start.13 = (bf16[64,1152]{1,0:T(8,128)(2,1)S(1)}, bf16[64,1152]{1,0:T(8,128)(2,1)S(1)}, u32[]{:S(2)}, u32[]{:S(2)}) collective-permute-start(bf16[64,1152]{1,0:T(8,128)(2,1)S(1)} %collective-permute-done.11.refs_1_), channel_id=1, source_target_pairs={{0,1},{1,0},{2,3},{3,2},{4,5},{5,4},{6,7},{7,6},{8,9},{9,8},{10,11... | collective-permute-start | bytes 442376 | tf_op jit(solution)/shard_map/ppermute | solution.py:365
  22.5 13.8 %collective-permute-start.7 = (bf16[64,1152]{1,0:T(8,128)(2,1)S(1)}, bf16[64,1152]{1,0:T(8,128)(2,1)S(1)}, u32[]{:S(2)}, u32[]{:S(2)}) collective-permute-start(bf16[64,1152]{1,0:T(8,128)(2,1)S(1)} %collective-permute-done.4.refs_0_), channel_id=1, source_target_pairs={{0,1},{1,0},{2,3},{3,2},{4,5},{5,4},{6,7},{7,6},{8,9},{9,8},{10,11... | collective-permute-start | bytes 442376 | tf_op jit(solution)/shard_map/ppermute | solution.py:365
  27.9 8.4 %collective-permute-start.8 = (bf16[64,1152]{1,0:T(8,128)(2,1)S(1)}, bf16[64,1152]{1,0:T(8,128)(2,1)S(1)}, u32[]{:S(2)}, u32[]{:S(2)}) collective-permute-start(bf16[64,1152]{1,0:T(8,128)(2,1)S(1)} %collective-permute-done.5.refs_1_), channel_id=1, source_target_pairs={{0,1},{1,0},{2,3},{3,2},{4,5},{5,4},{6,7},{7,6},{8,9},{9,8},{10,11... | collective-permute-start | bytes 442376 | tf_op jit(solution)/shard_map/ppermute | solution.py:365
  31.1 5.2 %collective-permute-start.9 = (bf16[64,1152]{1,0:T(8,128)(2,1)S(1)}, bf16[64,1152]{1,0:T(8,128)(2,1)S(1)}, u32[]{:S(2)}, u32[]{:S(2)}) collective-permute-start(bf16[64,1152]{1,0:T(8,128)(2,1)S(1)} %collective-permute-done.6.refs_2_), channel_id=1, source_target_pairs={{0,1},{1,0},{2,3},{3,2},{4,5},{5,4},{6,7},{7,6},{8,9},{9,8},{10,11... | collective-permute-start | bytes 442376 | tf_op jit(solution)/shard_map/ppermute | solution.py:365
  31.5 5.8 %collective-permute-start.2 = (bf16[64,1152]{1,0:T(8,128)(2,1)S(1)}, bf16[64,1152]{1,0:T(8,128)(2,1)S(1)}, u32[]{:S(2)}, u32[]{:S(2)}) collective-permute-start(bf16[64,1152]{1,0:T(8,128)(2,1)S(1)} %collective-permute-done.refs_0_), channel_id=1, source_target_pairs={{0,1},{1,0},{2,3},{3,2},{4,5},{5,4},{6,7},{7,6},{8,9},{9,8},{10,11... | collective-permute-start | bytes 442376 | tf_op jit(solution)/shard_map/ppermute | solution.py:365
  31.6 5.8 %collective-permute-start.3 = (bf16[64,1152]{1,0:T(8,128)(2,1)S(1)}, bf16[64,1152]{1,0:T(8,128)(2,1)S(1)}, u32[]{:S(2)}, u32[]{:S(2)}) collective-permute-start(bf16[64,1152]{1,0:T(8,128)(2,1)S(1)} %collective-permute-done.1.refs_1_), channel_id=1, source_target_pairs={{0,1},{1,0},{2,3},{3,2},{4,5},{5,4},{6,7},{7,6},{8,9},{9,8},{10,11... | collective-permute-start | bytes 442376 | tf_op jit(solution)/shard_map/ppermute | solution.py:365
